TPU v7x, 32 devices: a whole 2x2x4 slice. The times are simulated.
32 devices in a mesh: tm: 4 (over y, x), freq: 8 (over z, core).
Axes of the slice: x: 2, y: 2, z: 4, core: 2. Of those that a mesh axis runs over, the one named last changes fastest.
Arguments:
- records: bfloat16 [1024, 512, 512], P('freq', 'tm'), may hold values from -4 to 4
- gap_flags: int32 [1024, 16], P('freq', 'tm'), may hold values from -2147483648 to 2147483647
- station_mask: int32 [1024], P('freq'), may hold values 0 or 1
Outputs:
- cross_spectra: float32 [16, 2, 1024, 1024], P('freq', None, 'tm')
All inputs are finite; a program needn't handle non-finite values. No bound on the sum of `station_mask` on one device may be relied on, other than what follows from the above.
Results may differ from a plain program's by a relative error of at most 0.0013.
Values may be sent and summed in bfloat16 or wider, within the bound.
No kernel may reach another device: no remote copies, remote signals or barrier semaphores. Data moves between devices by JAX's collectives and lax.ppermute only.
A program may use at most 128 MiB of HBM per device.

v0:
```python
import math
import jax
import jax.numpy as jnp
from jax import lax
from jax.sharding import PartitionSpec as P

BAND_DEV = 2
FLOOR = 0.25


def transform_table(length, bin_count):
    sample_ids = jnp.arange(length, dtype=jnp.int32)
    bin_ids = jnp.arange(bin_count, dtype=jnp.int32)
    phase_ids = bin_ids[:, None] * sample_ids[None, :] % length
    angles = phase_ids.astype(jnp.float32) * (2.0 * math.pi / length)
    window_taper = 0.5 - 0.5 * jnp.cos(sample_ids.astype(jnp.float32) * (2.0 * math.pi / length))
    factor = window_taper / math.sqrt(length)
    dft_table = jnp.concatenate([jnp.cos(angles) * factor, -jnp.sin(angles) * factor], axis=0)
    return dft_table.astype(jnp.bfloat16)


def unpack_flags(packed_words):
    shifts = jnp.arange(32, dtype=jnp.int32)
    bit_values = jnp.bitwise_and(
        jnp.right_shift(packed_words[:, :, None], shifts[None, None, :]), 1
    )
    return bit_values.reshape(packed_words.shape[0], packed_words.shape[1] * 32)


def whiten(records, band_bins):
    bin_count = band_bins + 4
    dft_table = transform_table(records.shape[-1], bin_count)
    spectrum = jnp.einsum("cl,swl->scw", dft_table, records, preferred_element_type=jnp.float32)
    real_part = spectrum[:, :bin_count]
    imag_part = spectrum[:, bin_count:]
    magnitude = jnp.sqrt(real_part * real_part + imag_part * imag_part)
    smooth = (
        magnitude[:, 0:band_bins]
        + magnitude[:, 1 : band_bins + 1]
        + magnitude[:, 2 : band_bins + 2]
        + magnitude[:, 3 : band_bins + 3]
        + magnitude[:, 4 : band_bins + 4]
    ) / 5.0
    factor = 1.0 / jnp.maximum(smooth, FLOOR)
    whitened = jnp.stack(
        [real_part[:, 2 : band_bins + 2] * factor, imag_part[:, 2 : band_bins + 2] * factor], axis=2
    )
    return whitened.astype(jnp.bfloat16)


def block_terms(left_side, right_side):
    count_rows, bin_count, _, win_count = left_side.shape
    right_rows = right_side.shape[0]
    direct_left = left_side.reshape(count_rows, bin_count, 2 * win_count)
    turned_left = jnp.concatenate([left_side[:, :, 1], -left_side[:, :, 0]], axis=2)
    direct_right = right_side.reshape(right_rows, bin_count, 2 * win_count)
    real_part = jnp.einsum(
        "ifx,jfx->ifj", direct_left, direct_right, preferred_element_type=jnp.float32
    )
    imag_part = jnp.einsum(
        "ifx,jfx->ifj", turned_left, direct_right, preferred_element_type=jnp.float32
    )
    return jnp.stack([real_part, imag_part], axis=2).reshape(count_rows, 2 * bin_count, right_rows)


def local(records, gap_flags, station_mask):
    freq_size = lax.axis_size("freq")
    time_size = lax.axis_size("tm")
    band_bins = BAND_DEV * freq_size
    whitened = whiten(records, band_bins)
    kept_words = gap_flags * station_mask[:, None]
    spectra = lax.all_to_all(whitened, "freq", split_axis=1, concat_axis=0, tiled=True)
    all_words = lax.all_gather(kept_words, "freq", axis=0, tiled=True)
    here_flags = unpack_flags(all_words).astype(jnp.bfloat16)
    masked = spectra * here_flags[:, None, None, :]
    stations = spectra.shape[0]
    row_count = stations // time_size
    row_start = lax.axis_index("tm") * row_count
    every_words = lax.all_gather(all_words, "tm", axis=1, tiled=True)
    every_flags = unpack_flags(every_words).astype(jnp.bfloat16)
    row_flags = lax.dynamic_slice_in_dim(every_flags, row_start, row_count, 0)
    counts = jnp.dot(row_flags, every_flags.T, preferred_element_type=jnp.float32)
    window_part = lax.all_gather(masked, "tm", axis=3, tiled=True)
    left_side = lax.dynamic_slice_in_dim(window_part, row_start, row_count, 0)
    stacks = block_terms(left_side, window_part)
    divisor = jnp.maximum(counts, 1.0)
    result = stacks / divisor[:, None, :]
    return result.reshape(row_count, BAND_DEV, 2, stations).transpose(1, 2, 0, 3)


def solution(mesh):
    placed = (P("freq", "tm", None), P("freq", "tm"), P("freq"))
    return jax.shard_map(
        local, mesh=mesh, in_specs=placed, out_specs=P("freq", None, "tm", None), check_vma=False
    )
```

profile of v0, /device:TPU:0, one launch (start us, length us, event | category | flops | bytes accessed | tf_op | source)
XLA Modules:
  0.0 130.0 jit_solution(13890323300610356222)
XLA Ops:
  6.6 0.2 multiply_convert_fusion.1
  6.8 8.5 %convolution_bitcast_fusion = f32[128,40,128]{2,1,0:T(8,128)S(1)} fusion(bf16[128,128,512]{2,1,0:T(8,128)(2,1)} %param.3, bf16[20,512]{1,0:T(8,128)(2,1)S(1)} %get-tuple-element.10, bf16[20,512]{1,0:T(8,128)(2,1)S(1)} %get-tuple-element.9), kind=kOutput, calls=%fused_computation.5 | convolution fusion | flops 671170560 | bytes 19439616 | tf_op jit(solution)/shard_map/cl,swl->scw/dot_general | solution.py:33
  15.3 0.6 fusion.4
  15.9 0.7 fusion.13
  16.6 0.2 fusion.14
  16.9 1.2 copy.17
  18.2 6.3 %all-to-all-start = ((bf16[128,16,2,128]{3,0,2,1:T(8,128)(2,1)}), bf16[128,16,2,128]{3,0,2,1:T(8,128)(2,1)S(1)}, u32[]{:S(2)}, u32[]{:S(2)}) async-start(bf16[128,16,2,128]{3,0,2,1:T(8,128)(2,1)} %copy.17), calls=%async_computation | async-start | bytes 2097152 | tf_op jit(solution)/shard_map/all_to_all | solution.py:72
  24.7 32.5 %all_gather.9 = s32[1024,4]{0,1:T(4,128)S(1)} all-gather(s32[128,4]{0,1:T(4,128)S(1)} %broadcast_multiply_fusion), channel_id=1, replica_groups=mesh['tm'=4,'freq'=8] {'freq'}, dimensions={0}, use_global_device_ids=true | all-gather | bytes 18432 | tf_op jit(solution)/shard_map/all_gather | solution.py:73
  57.2 0.1 fusion.17
  57.3 0.2 copy.19
  57.6 1.1 bitcast_multiply_fusion
  58.8 8.2 %all-gather = s32[4,4,1024]{2,1,0:T(4,128)S(1)} all-gather(s32[1,4,1024]{2,1,0:T(4,128)S(1)} %bitcast.60), channel_id=1, replica_groups=mesh['tm'=4,'freq'=8] {'tm'}, dimensions={0}, use_global_device_ids=true | all-gather | bytes 81920 | tf_op jit(solution)/shard_map/all_gather | solution.py:79
  67.1 0.3 fusion.2
  67.4 0.5 convolution_maximum_fusion
  67.9 0.3 copy.22
  68.2 41.3 %all-gather.3.cloned.1.call-done = bf16[1024,2,2,512]{3,0,1,2:T(8,128)(2,1)} async-done(((bf16[1024,2,2,128]{3,0,1,2:T(8,128)(2,1)}), bf16[1024,2,2,512]{3,0,1,2:T(8,128)(2,1)}) %all-gather.3.cloned.1.call-update) | async-done | bytes 4194320 | tf_op jit(solution)/shard_map/all_gather | solution.py:83
  109.5 1.4 %dynamic-slice_bitcast_fusion = bf16[2,2,32,8,512]{4,3,2,1,0:T(8,128)(2,1)S(1)} fusion(bf16[1024,2,2,512]{3,0,1,2:T(8,128)(2,1)} %all-gather.3.cloned.1.call-done, s32[]{:T(128)S(6)} %select_n.14), kind=kLoop, calls=%fused_computation.29 | loop fusion | bytes 2097156
  111.0 0.1 copy.25
  111.1 0.9 copy-done
  112.1 0.6 copy.24
  112.7 1.3 %convolution_bitcast_fusion.2 = f32[256,2,1,1024]{0,3,1,2:T(8,128)S(1)} fusion(bf16[1024,2,1024]{2,0,1:T(8,128)(2,1)S(1)} %bitcast.54, bf16[256,2,1024]{2,0,1:T(8,128)(2,1)S(1)} %bitcast.57), kind=kOutput, calls=%fused_computation.7 | convolution fusion | flops 1073741824 | bytes 7340032 | tf_op jit(solution)/shard_map/ifx,jfx->ifj/dot_general | solution.py:57
  114.1 1.3 %convolution_bitcast_fusion.1 = f32[256,2,1,1024]{0,3,1,2:T(8,128)S(1)} fusion(bf16[1024,2,1024]{2,0,1:T(8,128)(2,1)S(1)} %bitcast.55, bf16[256,2,512]{2,0,1:T(8,128)(2,1)S(1)} %get-tuple-element.8, bf16[256,2,512]{2,0,1:T(8,128)(2,1)S(1)} %get-tuple-element.7), kind=kOutput, calls=%fused_computation.6 | convolution fusion | flops 1075838976 | bytes 7340032 | tf_op jit(solution)/shard_map/ifx,jfx->ifj/dot_general | solution.py:60
  115.5 2.3 %fusion = f32[2,2,256,1024]{2,3,0,1:T(8,128)} fusion(f32[256,2,1,1024]{0,3,1,2:T(8,128)S(1)} %convolution_bitcast_fusion.1, f32[256,2,1,1024]{0,3,1,2:T(8,128)S(1)} %convolution_bitcast_fusion.2, f32[256,1024]{0,1:T(8,128)S(1)} %copy.22), kind=kLoop, calls=%fused_computation.1 | loop fusion | flops 2097152 | bytes 9437184 | tf_op jit(solution)/shard_map/transpose | solution.py:88
  117.8 5.3 %copy.23 = f32[2,2,256,1024]{3,2,1,0:T(8,128)} copy(f32[2,2,256,1024]{2,3,0,1:T(8,128)} %fusion) | data formatting | bytes 8388608 | tf_op jit(solution)/shard_map/transpose | solution.py:88
  (18 shorter events, 0.6 us)
Async XLA Ops:
  16.9 7.8 %copy-start.1 = (s32[128,4]{0,1:T(4,128)S(1)}, s32[128,4]{0,1:T(4,128)}, u32[]{:S(2)}) copy-start(s32[128,4]{0,1:T(4,128)} %param.4) | copy-start | bytes 6148
  16.9 7.7 %copy-start.2 = (s32[128]{0:T(128)S(1)}, s32[128]{0:T(128)}, u32[]{:S(2)}) copy-start(s32[128]{0:T(128)} %param.5) | copy-start | bytes 1540
  18.2 39.3 %all-to-all-start = ((bf16[128,16,2,128]{3,0,2,1:T(8,128)(2,1)}), bf16[128,16,2,128]{3,0,2,1:T(8,128)(2,1)S(1)}, u32[]{:S(2)}, u32[]{:S(2)}) async-start(bf16[128,16,2,128]{3,0,2,1:T(8,128)(2,1)} %copy.17), calls=%async_computation | async-start | bytes 2097152 | tf_op jit(solution)/shard_map/all_to_all | solution.py:72
  24.5 85.0 %all-gather.3.cloned.1.call-start = ((), (), s32[]{:S(2)}) async-start(), calls=%async_computation.1 | async-start | bytes 5242880 | tf_op jit(solution)/shard_map/all_gather | solution.py:83
  109.5 2.5 %copy-start = (bf16[1024,2,2,512]{3,0,1,2:T(8,128)(2,1)S(1)}, bf16[1024,2,2,512]{3,0,1,2:T(8,128)(2,1)}, u32[]{:S(2)}) copy-start(bf16[1024,2,2,512]{3,0,1,2:T(8,128)(2,1)} %all-gather.3.cloned.1.call-done) | copy-start | bytes 12582916
Sparse Core Ops, SparseCore 0:
  58.9 50.6 all-gather.2
where the time goes:
time: 130 us
  waiting for transfers between devices  41.3 us (32%)
  blocking collectives  40.7 us (31%)
  between operations  13.6 us (10%)
  matrix products  11.6 us (9%)
  local copies, waits for them, and re-layouts  10.5 us (8%)
  starting transfers between devices  6.38 us (5%)
  other arithmetic  5.85 us (4%)
    all_gather x1, waiting for transfers between devices, local(): window_part = lax.all_gather(masked, 'tm', axis=3, tiled=True)  41.3 us
    all_gather x1, blocking collectives, local(): all_words = lax.all_gather(kept_words, 'freq', axis=0, tiled=True)  32.5 us
    dot_general x1, matrix products, whiten(): jnp.einsum('cl,swl->scw', dft_table, records, preferred_element_type=jnp....  8.47 us
    all_gather x1, blocking collectives, local(): every_words = lax.all_gather(all_words, 'tm', axis=1, tiled=True)  8.24 us
    all_to_all x1, starting transfers between devices, local(): lax.all_to_all(whitened, 'freq', split_axis=1, concat_axis=0, tiled=True)  6.35 us
    transpose x1, local copies, waits for them, and re-layouts, local(): result.reshape(row_count, BAND_DEV, 2, stations).transpose(1, 2, 0, 3)  5.34 us
  transfers between devices with their start and end apart: 2, of which 1 were waited for; matrix products, arithmetic and copies ran while one was open for 1% of the time, Pallas kernels for 0%

commit v1 on v0

--- a/solution.py
+++ b/solution.py
@@ -6,6 +6,19 @@
 
 BAND_DEV = 2
 FLOOR = 0.25
+
+
+def register_digits(w_in):
+    mesh_ax = "freq"
+    workers = lax.psum(1, mesh_ax)
+    all_rows = [None] * workers
+    all_rows[workers - 1] = w_in
+    found = [(tick, (tick + 1) % workers) for tick in range(workers)]
+    for u in range(workers - 2, -1, -1):
+        all_rows[u] = lax.ppermute(all_rows[u + 1], mesh_ax, found)
+    ready = jnp.concatenate(all_rows, 0)
+    x_now = lax.axis_index(mesh_ax)
+    return jnp.roll(ready, (x_now + 1) * w_in.shape[0], 0)
 
 
 def transform_table(length, bin_count):
@@ -70,7 +83,7 @@
     whitened = whiten(records, band_bins)
     kept_words = gap_flags * station_mask[:, None]
     spectra = lax.all_to_all(whitened, "freq", split_axis=1, concat_axis=0, tiled=True)
-    all_words = lax.all_gather(kept_words, "freq", axis=0, tiled=True)
+    all_words = register_digits(kept_words)
     here_flags = unpack_flags(all_words).astype(jnp.bfloat16)
     masked = spectra * here_flags[:, None, None, :]
     stations = spectra.shape[0]

time: 130 us -> 148 us (1.14)
  waiting for transfers between devices: 41.3 us -> 90.7 us
  blocking collectives: 40.7 us -> 8.73 us
    all_gather x1 -> x0, blocking collectives: 32.5 us -> none  [local(): all_words = lax.all_gather(kept_words, 'freq', axis=0, tiled=True)]
    all_to_all x1, waiting for transfers between devices: 0.01 us -> 25.9 us  [local(): lax.all_to_all(whitened, 'freq', split_axis=1, concat_axis=0, tiled=True)]
    ppermute x0 -> x7, waiting for transfers between devices: none -> 22.7 us  [register_digits(): all_rows[u] = lax.ppermute(all_rows[u + 1], mesh_ax, found)]
    all_to_all x1, starting transfers between devices: 6.35 us -> 4.82 us  [local(): lax.all_to_all(whitened, 'freq', split_axis=1, concat_axis=0, tiled=True)]
  transfers between devices with their start and end apart: 2 -> 9, of which waited for: 1 -> 7; matrix products, arithmetic and copies ran while one was open for 1% -> 9% of each run, Pallas kernels for 0% -> 0%
where the time goes in v1:
time: 148 us; the launch traced here: 147 us
  waiting for transfers between devices  90.7 us (61%)
  between operations  13.7 us (9%)
  matrix products  11.6 us (8%)
  local copies, waits for them, and re-layouts  10.6 us (7%)
  blocking collectives  8.73 us (6%)
  other arithmetic  6.56 us (4%)
  starting transfers between devices  5.42 us (4%)
    all_gather x1, waiting for transfers between devices, local(): window_part = lax.all_gather(masked, 'tm', axis=3, tiled=True)  42.1 us
    all_to_all x1, waiting for transfers between devices, local(): lax.all_to_all(whitened, 'freq', split_axis=1, concat_axis=0, tiled=True)  25.9 us
    ppermute x7, waiting for transfers between devices, register_digits(): all_rows[u] = lax.ppermute(all_rows[u + 1], mesh_ax, found)  22.7 us
    all_gather x1, blocking collectives, local(): every_words = lax.all_gather(all_words, 'tm', axis=1, tiled=True)  8.73 us
    dot_general x1, matrix products, whiten(): jnp.einsum('cl,swl->scw', dft_table, records, preferred_element_type=jnp....  8.46 us
    transpose x1, local copies, waits for them, and re-layouts, local(): result.reshape(row_count, BAND_DEV, 2, stations).transpose(1, 2, 0, 3)  5.34 us
    all_to_all x1, starting transfers between devices, local(): lax.all_to_all(whitened, 'freq', split_axis=1, concat_axis=0, tiled=True)  4.82 us
  transfers between devices with their start and end apart: 9, of which 7 were waited for; matrix products, arithmetic and copies ran while one was open for 9% of the time, Pallas kernels for 0%

profile of v1, /device:TPU:0, one launch (start us, length us, event | category | flops | bytes accessed | tf_op | source)
XLA Modules:
  0.0 147.3 jit_solution(493992318661960791)
XLA Ops:
  6.5 0.7 broadcast_multiply_fusion
  7.2 0.5 collective-permute-start
  7.8 5.2 %collective-permute-done = s32[128,4]{0,1:T(4,128)S(1)} collective-permute-done((s32[128,4]{0,1:T(4,128)S(1)}, s32[128,4]{0,1:T(4,128)S(1)}, u32[]{:S(2)}, u32[]{:S(2)}) %collective-permute-start) | collective-permute-done | bytes 2080 | tf_op jit(solution)/shard_map/ppermute | solution.py:18
  13.2 4.6 %collective-permute-done.1 = s32[128,4]{0,1:T(4,128)S(1)} collective-permute-done((s32[128,4]{0,1:T(4,128)S(1)}, s32[128,4]{0,1:T(4,128)S(1)}, u32[]{:S(2)}, u32[]{:S(2)}) %collective-permute-start.1) | collective-permute-done | bytes 2080 | tf_op jit(solution)/shard_map/ppermute | solution.py:18
  17.8 8.5 %convolution_bitcast_fusion = f32[128,40,128]{2,1,0:T(8,128)S(1)} fusion(bf16[128,128,512]{2,1,0:T(8,128)(2,1)} %param.3, bf16[20,512]{1,0:T(8,128)(2,1)S(1)} %get-tuple-element.10, bf16[20,512]{1,0:T(8,128)(2,1)S(1)} %get-tuple-element.9), kind=kOutput, calls=%fused_computation.5 | convolution fusion | flops 671170560 | bytes 19439616 | tf_op jit(solution)/shard_map/cl,swl->scw/dot_general | solution.py:46
  26.4 0.6 fusion.4
  27.0 4.2 %collective-permute-done.3 = s32[128,4]{0,1:T(4,128)S(1)} collective-permute-done((s32[128,4]{0,1:T(4,128)S(1)}, s32[128,4]{0,1:T(4,128)S(1)}, u32[]{:S(2)}, u32[]{:S(2)}) %collective-permute-start.3) | collective-permute-done | bytes 2080 | tf_op jit(solution)/shard_map/ppermute | solution.py:18
  31.2 0.7 fusion.13
  31.9 4.1 %collective-permute-done.4 = s32[128,4]{0,1:T(4,128)S(1)} collective-permute-done((s32[128,4]{0,1:T(4,128)S(1)}, s32[128,4]{0,1:T(4,128)S(1)}, u32[]{:S(2)}, u32[]{:S(2)}) %collective-permute-start.4) | collective-permute-done | bytes 2080 | tf_op jit(solution)/shard_map/ppermute | solution.py:18
  36.2 4.6 %collective-permute-done.5 = s32[128,4]{0,1:T(4,128)S(1)} collective-permute-done((s32[128,4]{0,1:T(4,128)S(1)}, s32[128,4]{0,1:T(4,128)S(1)}, u32[]{:S(2)}, u32[]{:S(2)}) %collective-permute-start.5) | collective-permute-done | bytes 2080 | tf_op jit(solution)/shard_map/ppermute | solution.py:18
  40.9 1.2 copy.17
  42.2 4.8 %all-to-all-start = ((bf16[128,16,2,128]{3,0,2,1:T(8,128)(2,1)}), bf16[128,16,2,128]{3,0,2,1:T(8,128)(2,1)S(1)}, u32[]{:S(2)}, u32[]{:S(2)}) async-start(bf16[128,16,2,128]{3,0,2,1:T(8,128)(2,1)} %copy.17), calls=%async_computation | async-start | bytes 2097152 | tf_op jit(solution)/shard_map/all_to_all | solution.py:85
  47.7 25.9 %all-to-all-done = bf16[128,16,2,128]{3,0,2,1:T(8,128)(2,1)S(1)} async-done(((bf16[128,16,2,128]{3,0,2,1:T(8,128)(2,1)}), bf16[128,16,2,128]{3,0,2,1:T(8,128)(2,1)S(1)}, u32[]{:S(2)}, u32[]{:S(2)}) %all-to-all-start) | async-done | bytes 1048608 | tf_op jit(solution)/shard_map/all_to_all | solution.py:85
  73.6 1.1 bitcast_multiply_fusion
  74.9 8.7 %all-gather = s32[4,4,1024]{2,1,0:T(4,128)S(1)} all-gather(s32[1,4,1024]{2,1,0:T(4,128)S(1)} %fusion.36), channel_id=1, replica_groups=mesh['tm'=4,'freq'=8] {'tm'}, dimensions={0}, use_global_device_ids=true | all-gather | bytes 81920 | tf_op jit(solution)/shard_map/all_gather | solution.py:92
  83.9 0.5 convolution_maximum_fusion
  84.8 42.1 %all-gather.3.cloned.1.call-done = bf16[1024,2,2,512]{3,0,1,2:T(8,128)(2,1)} async-done(((bf16[1024,2,2,128]{3,0,1,2:T(8,128)(2,1)}), bf16[1024,2,2,512]{3,0,1,2:T(8,128)(2,1)}) %all-gather.3.cloned.1.call-update) | async-done | bytes 4194320 | tf_op jit(solution)/shard_map/all_gather | solution.py:96
  126.9 1.4 dynamic-slice_bitcast_fusion
  128.4 0.9 copy-done
  129.4 0.6 copy.24
  130.0 1.3 convolution_bitcast_fusion.2
  131.4 1.3 convolution_bitcast_fusion.1
  132.8 2.3 %fusion = f32[2,2,256,1024]{2,3,0,1:T(8,128)} fusion(f32[256,2,1,1024]{0,3,1,2:T(8,128)S(1)} %convolution_bitcast_fusion.1, f32[256,2,1,1024]{0,3,1,2:T(8,128)S(1)} %convolution_bitcast_fusion.2, f32[256,1024]{0,1:T(8,128)S(1)} %copy.22), kind=kLoop, calls=%fused_computation.1 | loop fusion | flops 2097152 | bytes 9437184 | tf_op jit(solution)/shard_map/transpose | solution.py:101
  135.1 5.3 %copy.23 = f32[2,2,256,1024]{3,2,1,0:T(8,128)} copy(f32[2,2,256,1024]{2,3,0,1:T(8,128)} %fusion) | data formatting | bytes 8388608 | tf_op jit(solution)/shard_map/transpose | solution.py:101
  (49 shorter events, 2.3 us)
Async XLA Ops:
  7.2 5.8 %collective-permute-start = (s32[128,4]{0,1:T(4,128)S(1)}, s32[128,4]{0,1:T(4,128)S(1)}, u32[]{:S(2)}, u32[]{:S(2)}) collective-permute-start(s32[128,4]{0,1:T(4,128)S(1)} %broadcast_multiply_fusion), channel_id=1, source_target_pairs={{0,1},{1,2},{2,3},{3,4},{4,5},{5,6},{6,7},{7,0},{8,9},{9,10},{10,1... | collective-permute-start | bytes 6152 | tf_op jit(solution)/shard_map/ppermute | solution.py:18
  13.0 4.8 %collective-permute-start.1 = (s32[128,4]{0,1:T(4,128)S(1)}, s32[128,4]{0,1:T(4,128)S(1)}, u32[]{:S(2)}, u32[]{:S(2)}) collective-permute-start(s32[128,4]{0,1:T(4,128)S(1)} %collective-permute-done), channel_id=1, source_target_pairs={{0,1},{1,2},{2,3},{3,4},{4,5},{5,6},{6,7},{7,0},{8,9},{9,10},{10,1... | collective-permute-start | bytes 6152 | tf_op jit(solution)/shard_map/ppermute | solution.py:18
  17.8 8.5 %collective-permute-start.2 = (s32[128,4]{0,1:T(4,128)S(1)}, s32[128,4]{0,1:T(4,128)S(1)}, u32[]{:S(2)}, u32[]{:S(2)}) collective-permute-start(s32[128,4]{0,1:T(4,128)S(1)} %collective-permute-done.1), channel_id=1, source_target_pairs={{0,1},{1,2},{2,3},{3,4},{4,5},{5,6},{6,7},{7,0},{8,9},{9,10},{10,1... | collective-permute-start | bytes 6152 | tf_op jit(solution)/shard_map/ppermute | solution.py:18
  26.3 4.9 %collective-permute-start.3 = (s32[128,4]{0,1:T(4,128)S(1)}, s32[128,4]{0,1:T(4,128)S(1)}, u32[]{:S(2)}, u32[]{:S(2)}) collective-permute-start(s32[128,4]{0,1:T(4,128)S(1)} %collective-permute-done.2), channel_id=1, source_target_pairs={{0,1},{1,2},{2,3},{3,4},{4,5},{5,6},{6,7},{7,0},{8,9},{9,10},{10,1... | collective-permute-start | bytes 6152 | tf_op jit(solution)/shard_map/ppermute | solution.py:18
  31.2 4.8 %collective-permute-start.4 = (s32[128,4]{0,1:T(4,128)S(1)}, s32[128,4]{0,1:T(4,128)S(1)}, u32[]{:S(2)}, u32[]{:S(2)}) collective-permute-start(s32[128,4]{0,1:T(4,128)S(1)} %collective-permute-done.3), channel_id=1, source_target_pairs={{0,1},{1,2},{2,3},{3,4},{4,5},{5,6},{6,7},{7,0},{8,9},{9,10},{10,1... | collective-permute-start | bytes 6152 | tf_op jit(solution)/shard_map/ppermute | solution.py:18
  36.0 4.8 %collective-permute-start.5 = (s32[128,4]{0,1:T(4,128)S(1)}, s32[128,4]{0,1:T(4,128)S(1)}, u32[]{:S(2)}, u32[]{:S(2)}) collective-permute-start(s32[128,4]{0,1:T(4,128)S(1)} %collective-permute-done.4), channel_id=1, source_target_pairs={{0,1},{1,2},{2,3},{3,4},{4,5},{5,6},{6,7},{7,0},{8,9},{9,10},{10,1... | collective-permute-start | bytes 6152 | tf_op jit(solution)/shard_map/ppermute | solution.py:18
  40.8 6.3 %collective-permute-start.6 = (s32[128,4]{0,1:T(4,128)S(1)}, s32[128,4]{0,1:T(4,128)S(1)}, u32[]{:S(2)}, u32[]{:S(2)}) collective-permute-start(s32[128,4]{0,1:T(4,128)S(1)} %collective-permute-done.5), channel_id=1, source_target_pairs={{0,1},{1,2},{2,3},{3,4},{4,5},{5,6},{6,7},{7,0},{8,9},{9,10},{10,1... | collective-permute-start | bytes 6152 | tf_op jit(solution)/shard_map/ppermute | solution.py:18
  40.9 6.3 %copy-start.1 = (s32[128,4]{0,1:T(4,128)S(1)}, s32[128,4]{0,1:T(4,128)}, u32[]{:S(2)}) copy-start(s32[128,4]{0,1:T(4,128)} %param.4) | copy-start | bytes 6148
  40.9 6.3 %copy-start.2 = (s32[128]{0:T(128)S(1)}, s32[128]{0:T(128)}, u32[]{:S(2)}) copy-start(s32[128]{0:T(128)} %param.5) | copy-start | bytes 1540
  42.2 31.4 %all-to-all-start = ((bf16[128,16,2,128]{3,0,2,1:T(8,128)(2,1)}), bf16[128,16,2,128]{3,0,2,1:T(8,128)(2,1)S(1)}, u32[]{:S(2)}, u32[]{:S(2)}) async-start(bf16[128,16,2,128]{3,0,2,1:T(8,128)(2,1)} %copy.17), calls=%async_computation | async-start | bytes 2097152 | tf_op jit(solution)/shard_map/all_to_all | solution.py:85
  47.0 79.9 %all-gather.3.cloned.1.call-start = ((), (), s32[]{:S(2)}) async-start(), calls=%async_computation.1 | async-start | bytes 5242880 | tf_op jit(solution)/shard_map/all_gather | solution.py:96
  126.8 2.5 %copy-start = (bf16[1024,2,2,512]{3,0,1,2:T(8,128)(2,1)S(1)}, bf16[1024,2,2,512]{3,0,1,2:T(8,128)(2,1)}, u32[]{:S(2)}) copy-start(bf16[1024,2,2,512]{3,0,1,2:T(8,128)(2,1)} %all-gather.3.cloned.1.call-done) | copy-start | bytes 12582916
Sparse Core Ops, SparseCore 0:
  74.9 51.9 all-gather.2
